TPU v7x, 32 devices: a whole 2x2x4 slice. The times are simulated.
32 devices in a mesh: illum: 2 (over x), box: 16 (over z, y, core).
Axes of the slice: x: 2, y: 2, z: 4, core: 2. Of those that a mesh axis runs over, the one named last changes fastest.
Arguments:
- patterns: bfloat16 [2, 256, 128, 256], P(None, 'box', None, 'illum'), parts along dimension 3, may hold values from -6 to 6
- owner_block: int32 [4], replicated, may hold values from 0 to 31
- low_index: int32 [256, 48], P('box'), may hold values from 0 to 315
- low_mask: int32 [256, 48], P('box'), may hold values 0 or 1
- low_table: bfloat16 [2, 316, 128], replicated, may hold values from -2 to 2
- interp: bfloat16 [128, 512], replicated, may hold values from -0.5 to 0.5
- shift_angle: float32 [8, 512], replicated, may hold values from -3.140625 to 3.140625
- par_source: int32 [32, 16], replicated, may hold values from 0 to 31, as said below
- par_index: int32 [32, 16], replicated, may hold values from 0 to 315
- par_mask: int32 [32, 16], replicated, may hold values 0 or 1
- par_table: bfloat16 [2, 316, 512], replicated, may hold values from -1.5 to 1.5
Outputs:
- incoming: float32 [2, 256, 128, 256], P(None, 'box', None, 'illum'), parts along dimension 3
There are 2 independent parts, one for each index of `illum`. A program takes and returns all parts, laid end to end along the dimension named above; an argument that names none is the same for every part. Nothing has to cross between parts.
Inputs may be any that keep to these rules, and one draw needn't show every extreme that they name: `par_source`: each parent's 16 slots name distinct parents other than itself.
All inputs are finite; a program needn't handle non-finite values. No bound on the sum of `low_mask` on one device may be relied on, other than what follows from the above.
Results may differ from a plain program's by a relative error of at most 0.0047.
Values may be sent and summed in bfloat16 or wider, within the bound.
A program may use at most 64 MiB of HBM per device.

v0:
```python
import jax
import jax.numpy as jnp
from jax import lax
from jax.sharding import PartitionSpec as P


def broadcast(x, axis, root):
    mine = lax.axis_index(axis) == root
    return lax.psum(jnp.where(mine, x, jnp.zeros_like(x)), axis)


def complex_apply(operator, sources):

    def single(left, right):
        return jnp.einsum("bjk,jkr->bkr", left, right, preferred_element_type=jnp.float32)

    real_part = single(operator[0], sources[0]) - single(operator[1], sources[1])
    imaginary = single(operator[0], sources[1]) + single(operator[1], sources[0])
    return jnp.stack([real_part, imaginary])


def shards(
    patterns,
    owner_block,
    low_index,
    low_mask,
    low_table,
    interp,
    shift_angle,
    par_source,
    par_index,
    par_mask,
    par_table,
):
    box_dev = patterns.shape[1]
    blocks_each = box_dev // 8
    directions = interp.shape[1]
    illums = patterns.shape[3]
    groups = lax.axis_size("box")
    listed = owner_block.shape[0]
    cosine = jnp.cos(shift_angle)[None, :, :, None]
    sine = jnp.sin(shift_angle)[None, :, :, None]
    operator = low_table[:, low_index] * low_mask[None, :, :, None].astype(jnp.bfloat16)
    early = complex_apply(operator[:, :, :box_dev], patterns)
    pieces = []
    for listed_step in range(listed):
        owner = owner_block[listed_step]
        local_block = lax.dynamic_slice_in_dim(patterns, owner % blocks_each * 8, 8, 1)
        pieces.append(broadcast(local_block, "box", owner // blocks_each))
    far_boxes = jnp.concatenate(pieces, axis=1)
    near = early + complex_apply(operator[:, :, box_dev:], far_boxes)
    lifted = jnp.einsum("cbkr,kq->cbqr", patterns, interp, preferred_element_type=jnp.float32)
    lifted = lifted.reshape(2, blocks_each, 8, directions, illums)
    real_part = jnp.sum(cosine * lifted[0] - sine * lifted[1], axis=1)
    imaginary = jnp.sum(cosine * lifted[1] + sine * lifted[0], axis=1)
    parent_local = jnp.stack([real_part, imaginary]).astype(jnp.bfloat16)
    parents_total = par_source.shape[0]
    dir_local = directions // groups
    dir_start = lax.axis_index("box") * dir_local
    table_slice = lax.dynamic_slice_in_dim(par_table, dir_start, dir_local, 2)
    rows = table_slice[:, par_index]
    selector = (
        (par_source[:, :, None] == jnp.arange(parents_total, dtype=jnp.int32)[None, None, :])
        & (par_mask[:, :, None] > 0)
    ).astype(jnp.bfloat16)
    coupling = jnp.einsum(
        "pjs,cpjq->cqps", selector, rows, preferred_element_type=jnp.float32
    ).astype(jnp.bfloat16)
    block = lax.all_to_all(parent_local, "box", split_axis=2, concat_axis=1, tiled=True)

    def single(left, right):
        return jnp.einsum("qps,sqr->pqr", left, right, preferred_element_type=jnp.float32)

    real_out = single(coupling[0], block[0]) - single(coupling[1], block[1])
    imag_out = single(coupling[0], block[1]) + single(coupling[1], block[0])
    result = jnp.stack([real_out, imag_out]).astype(jnp.bfloat16)
    translated = lax.all_to_all(result, "box", split_axis=1, concat_axis=2, tiled=True)
    wide = translated.astype(jnp.float32)[:, :, None]
    real_down = cosine * wide[0] + sine * wide[1]
    imag_down = cosine * wide[1] - sine * wide[0]
    phased = (
        jnp.stack([real_down, imag_down])
        .astype(jnp.bfloat16)
        .reshape(2, box_dev, directions, illums)
    )
    down = jnp.einsum("cbqr,kq->cbkr", phased, interp, preferred_element_type=jnp.float32)
    return near + down


def solution(mesh):
    placed = (
        P(None, "box", None, "illum"),
        P(),
        P("box", None),
        P("box", None),
        P(),
        P(),
        P(),
        P(),
        P(),
        P(),
        P(),
    )
    return jax.shard_map(
        shards, mesh=mesh, in_specs=placed, out_specs=P(None, "box", None, "illum"), check_vma=False
    )
```

profile of v0, /device:TPU:0, one launch (start us, length us, event | category | flops | bytes accessed | tf_op | source)
XLA Modules:
  0.0 168.8 jit_solution(7000459136940673514)
XLA Ops:
  7.4 2.6 %convolution_bitcast_fusion = f32[2,16,512,128]{3,2,1,0:T(8,128)S(1)} fusion(bf16[2,16,128,128]{3,2,1,0:T(8,128)(2,1)} %param.11, bf16[128,512]{1,0:T(8,128)(2,1)} %param.16), kind=kOutput, calls=%fused_computation.16 | convolution fusion | flops 536870912 | bytes 9568256 | tf_op jit(solution)/shard_map/cbkr,kq->cbqr/dot_general | solution.py:52
  10.9 1.6 subtract_reduce_fusion
  12.6 1.3 copy.138
  14.0 7.4 %all-to-all-start = ((bf16[2,2,512,128]{3,1,0,2:T(2,128)(2,1)}), bf16[2,2,512,128]{3,1,0,2:T(2,128)(2,1)S(1)}, u32[]{:S(2)}, u32[]{:S(2)}) async-start(bf16[2,2,512,128]{3,1,0,2:T(2,128)(2,1)} %copy.138), calls=%async_computation | async-start | bytes 1048576 | tf_op jit(solution)/shard_map/all_to_all | solution.py:69
  33.1 1.7 copy_select_fusion
  34.7 1.7 copy_select_fusion.2
  37.6 2.9 %gather_fusion = bf16[768,2,128]{2,1,0:T(2,128)(2,1)S(1)} fusion(bf16[2,316,128]{2,0,1:T(2,128)(2,1)S(1)} %copy-done.3, s32[1024]{0:T(1024)S(1)} %get-tuple-element.34), kind=kCustom, calls=%fused_computation | custom fusion | bytes 789504 | tf_op jit(solution)/shard_map/gather | solution.py:43
  40.5 1.4 copy.130
  41.9 1.3 multiply_bitcast_fusion
  43.7 1.5 fusion.21
  45.1 1.5 fusion.12
  46.8 2.1 %gather_fusion.1 = bf16[512,2,32]{2,1,0:T(2,128)(2,1)S(1)} fusion(bf16[2,316,32]{2,0,1:T(2,128)(2,1)S(1)} %constant_dynamic-slice_fusion, s32[1024]{0:T(1024)S(1)} %get-tuple-element.33), kind=kCustom, calls=%fused_computation.1 | custom fusion | bytes 133120 | tf_op jit(solution)/shard_map/gather | solution.py:61
  49.0 2.8 %fusion.11 = f32[1,16,128,128]{3,1,2,0:T(8,128)} fusion(f32[128,16,128]{2,1,0:T(8,128)} %fusion.21, bf16[1,16,128,128]{3,2,1,0:T(8,128)(2,1)S(1)} %get-tuple-element.21, bf16[2,16,48,128]{2,1,3,0:T(8,128)(2,1)S(1)} %multiply_bitcast_fusion), kind=kOutput, calls=%fused_computation.24 | convolution fusion | flops 8650752 | bytes 3145728 | tf_op jit(solution)/shard_map/bjk,jkr->bkr/dot_general | solution.py:15
  55.0 6.0 %all-to-all-start.1 = ((bf16[2,32,32,128]{3,2,0,1:T(8,128)(2,1)}), bf16[2,32,32,128]{3,2,0,1:T(8,128)(2,1)S(1)}, u32[]{:S(2)}, u32[]{:S(2)}) async-start(bf16[2,32,32,128]{3,2,0,1:T(8,128)(2,1)} %copy.150), calls=%async_computation.1 | async-start | bytes 1048576 | tf_op jit(solution)/shard_map/all_to_all | solution.py:77
  61.0 81.3 %all-reduce.3.cloned.1.call-done = (bf16[2,8,128,128]{3,1,2,0:T(8,128)(2,1)}, bf16[2,8,128,128]{3,1,2,0:T(8,128)(2,1)}, bf16[2,8,128,128]{3,1,2,0:T(8,128)(2,1)}, bf16[2,8,128,128]{3,1,2,0:T(8,128)(2,1)}) async-done(((bf16[2,8,128,128]{3,1,2,0:T(8,128)(2,1)}, bf16[2,8,128,128]{3,1,2,0:T(8,128)(2,1)}, bf16[2,8,128,128]{3,1,2,0:T(8,128)(2,1)}, bf16[2,8,128,128]{3,1,2,0:T(8,128)(2,1)}), ...) | async-done | bytes 2097168 | tf_op jit(solution)/shard_map/psum | solution.py:9
  142.3 1.2 constant_dynamic-update-slice_fusion.3
  143.6 1.2 constant_dynamic-update-slice_fusion.2
  145.5 1.5 fusion.10
  147.5 1.5 fusion.9
  150.8 1.6 fusion.1
  152.4 2.6 %fusion.4 = f32[2,16,128,128]{3,2,1,0:T(8,128)} fusion(bf16[1,16,512,128]{2,3,1,0:T(8,128)(2,1)S(1)} %get-tuple-element.12, bf16[1,16,512,128]{2,3,1,0:T(8,128)(2,1)S(1)} %get-tuple-element.11, bf16[128,512]{1,0:T(8,128)(2,1)S(1)} %copy-done.6), kind=kOutput, calls=%fused_computation.10 | convolution fusion | flops 538968064 | bytes 6422528 | tf_op jit(solution)/shard_map/cbqr,kq->cbkr/dot_general | solution.py:86
  155.0 2.2 %copy.156 = f32[2,16,128,128]{2,1,3,0:T(8,128)S(1)} copy(f32[2,16,128,128]{3,2,1,0:T(8,128)} %fusion.4) | data formatting | bytes 4194304 | tf_op jit(solution)/shard_map/cbqr,kq->cbkr/dot_general | solution.py:86
  157.3 2.7 %fusion.8 = f32[2,16,128,128]{3,1,2,0:T(8,128)S(1)} fusion(f32[1,16,128,128]{3,1,2,0:T(8,128)} %fusion.11, f32[1,16,128,128]{3,1,2,0:T(8,128)} %fusion.12, f32[1,16,128,128]{3,1,2,0:T(8,128)} %fusion.9, f32[1,16,128,128]{3,1,2,0:T(8,128)} %fusion.10, f32[2,16,128,128]{2,1,3,0:T(8,128)S(1)} %copy.156), kind=kLoop, calls=%fused_computation.18 | loop fusion | flops 2097152 | bytes 8388608 | tf_op jit(solution)/shard_map/add | solution.py:87
  160.0 1.9 %copy.157 = f32[2,16,128,128]{3,2,1,0:T(8,128)} copy(f32[2,16,128,128]{3,1,2,0:T(8,128)S(1)} %fusion.8) | data formatting | bytes 4194304 | tf_op jit(solution)/shard_map/add | solution.py:87
  (74 shorter events, 10.8 us)
Async XLA Ops:
  6.5 40.1 %copy-start = (bf16[2,316,512]{2,0,1:T(2,128)(2,1)S(1)}, bf16[2,316,512]{2,0,1:T(2,128)(2,1)}, u32[]{:S(2)}) copy-start(bf16[2,316,512]{2,0,1:T(2,128)(2,1)} %param.21) | copy-start | bytes 1941508
  12.5 8.9 %copy-start.12 = (s32[4]{0:T(128)S(1)}, s32[4]{0:T(128)}, u32[]{:S(2)}) copy-start(s32[4]{0:T(128)} %param.12) | copy-start | bytes 52
  12.5 20.3 %copy-start.2 = (bf16[2,16,128,128]{3,2,1,0:T(8,128)(2,1)S(1)}, bf16[2,16,128,128]{3,2,1,0:T(8,128)(2,1)}, u32[]{:S(2)}) copy-start(bf16[2,16,128,128]{3,2,1,0:T(8,128)(2,1)} %param.11) | copy-start | bytes 3145732
  14.0 38.3 %all-to-all-start = ((bf16[2,2,512,128]{3,1,0,2:T(2,128)(2,1)}), bf16[2,2,512,128]{3,1,0,2:T(2,128)(2,1)S(1)}, u32[]{:S(2)}, u32[]{:S(2)}) async-start(bf16[2,2,512,128]{3,1,0,2:T(2,128)(2,1)} %copy.138), calls=%async_computation | async-start | bytes 1048576 | tf_op jit(solution)/shard_map/all_to_all | solution.py:69
  21.4 120.9 %all-reduce.3.cloned.1.call-start = ((), (), s32[]{:S(2)}) async-start(), calls=%async_computation.2 | async-start | bytes 4194304 | tf_op jit(solution)/shard_map/psum | solution.py:9
  36.4 0.7 copy-start.10
  36.4 0.9 copy-start.11
  36.4 0.9 copy-start.7
  36.4 1.0 copy-start.8
  36.4 1.1 copy-start.3
  36.5 5.4 %copy-start.9 = (s32[16,48]{1,0:T(8,128)S(1)}, s32[16,48]{1,0:T(8,128)}, u32[]{:S(2)}) copy-start(s32[16,48]{1,0:T(8,128)} %param.14) | copy-start | bytes 9220
  55.0 94.0 %all-to-all-start.1 = ((bf16[2,32,32,128]{3,2,0,1:T(8,128)(2,1)}), bf16[2,32,32,128]{3,2,0,1:T(8,128)(2,1)S(1)}, u32[]{:S(2)}, u32[]{:S(2)}) async-start(bf16[2,32,32,128]{3,2,0,1:T(8,128)(2,1)} %copy.150), calls=%async_computation.1 | async-start | bytes 1048576 | tf_op jit(solution)/shard_map/all_to_all | solution.py:77
  142.3 2.4 %copy-start.5 = (bf16[2,8,128,128]{3,1,2,0:T(8,128)(2,1)S(1)}, bf16[2,8,128,128]{3,1,2,0:T(8,128)(2,1)}, u32[]{:S(2)}) copy-start(bf16[2,8,128,128]{3,1,2,0:T(8,128)(2,1)} %get-tuple-element.9) | copy-start | bytes 1572868
  142.3 2.5 %copy-start.4 = (bf16[2,8,128,128]{3,1,2,0:T(8,128)(2,1)S(1)}, bf16[2,8,128,128]{3,1,2,0:T(8,128)(2,1)}, u32[]{:S(2)}) copy-start(bf16[2,8,128,128]{3,1,2,0:T(8,128)(2,1)} %get-tuple-element.10) | copy-start | bytes 1572868
  150.8 1.6 copy-start.6
  157.3 4.7 %copy-start.1 = (bf16[2,316,512]{2,0,1:T(2,128)(2,1)S(1)}, bf16[2,316,512]{2,0,1:T(2,128)(2,1)}, u32[]{:S(2)}) copy-start(bf16[2,316,512]{2,0,1:T(2,128)(2,1)} %param.21) | copy-start | bytes 1941508
Sparse Core Ops, SparseCore 0:
  36.6 105.7 all-reduce.2
where the time goes:
time: 169 us
  waiting for transfers between devices  81.4 us (48%)
  between operations  24.5 us (14%)
  local copies, waits for them, and re-layouts  21.9 us (13%)
  matrix products  16.7 us (10%)
  starting transfers between devices  13.5 us (8%)
  other arithmetic  10.9 us (6%)
    psum x1, waiting for transfers between devices, broadcast(): return lax.psum(jnp.where(mine, x, jnp.zeros_like(x)), axis)  81.3 us
    dot_general x8, matrix products, single(): jnp.einsum('bjk,jkr->bkr', left, right, preferred_element_type=jnp.float32)  10.1 us
    all_to_all x1, starting transfers between devices, shards(): lax.all_to_all(parent_local, 'box', split_axis=2, concat_axis=1, tiled=True)  7.41 us
    all_to_all x1, starting transfers between devices, shards(): lax.all_to_all(result, 'box', split_axis=1, concat_axis=2, tiled=True)  6 us
    gather x2, local copies, waits for them, and re-layouts, shards(): low_table[:, low_index] * low_mask[None, :, :, None].astype(jnp.bfloat16)  4.33 us
  transfers between devices with their start and end apart: 3, of which 1 were waited for; matrix products, arithmetic and copies ran while one was open for 17% of the time, Pallas kernels for 0%

commit v1 on v0

v1 whole, which is shorter than its diff:
```python
import functools

import jax
import jax.numpy as jnp
from jax import lax
from jax.experimental import pallas as pl
from jax.experimental.pallas import tpu as pltpu
from jax.sharding import PartitionSpec as P

F32 = jnp.float32
BF16 = jnp.bfloat16
MESH = pl.DeviceIdType.MESH


def dot(left, right):
    return jnp.dot(left, right, preferred_element_type=F32)


def kernel(
    n,
    listed,
    owner_ref,
    pat_ref,
    own_op_ref,
    far_op_ref,
    interp_ref,
    lift_ref,
    phase_ref,
    couple_ref,
    out_ref,
    parent,
    arrived,
    wide,
    result,
    result_send,
    returned,
    buf,
    landed,
    far,
    far_wide,
    own_wide,
    acc,
    out_send,
    out_recv,
    back_send,
    back_recv,
    rs_send,
    rs_recv,
    ag_send,
    ag_recv,
):
    me = lax.axis_index("box")
    boxes = pat_ref.shape[1]
    kdir, illums = pat_ref.shape[2], pat_ref.shape[3]
    groups8 = boxes // 8
    qdir = lift_ref.shape[0]
    qloc = qdir // n
    rows = 2 * listed * 8
    stages = n.bit_length() - 1

    barrier = pltpu.get_barrier_semaphore()

    def greet(i, carry):
        peer = lax.rem(me + i, n)
        pl.semaphore_signal(barrier, inc=1, device_id={"box": peer}, device_id_type=MESH)
        return carry

    lax.fori_loop(1, n, greet, 0)

    for step in range(listed):
        owner = owner_ref[step]
        mine = owner // groups8 == me
        first = owner % groups8 * 8
        for part in range(2):
            block = pat_ref[part, pl.ds(first, 8)]
            buf[pl.ds((part * listed + step) * 8, 8)] = jnp.where(mine, block, jnp.zeros_like(block))

    pl.semaphore_wait(barrier, n - 1)

    def halving(stage):
        size = rows >> (stage + 1)
        low = 0
        for s in range(stage):
            low = low + (me // (1 << s) % 2) * (rows >> (s + 1))
        bit = me // (1 << stage) % 2
        keep = low + bit * size
        give = low + (1 - bit) * size
        partner = me + (1 - 2 * bit) * (1 << stage)
        spot = rows - 2 * size
        copy = pltpu.make_async_remote_copy(
            src_ref=buf.at[pl.ds(give, size)],
            dst_ref=landed.at[pl.ds(spot, size)],
            send_sem=rs_send.at[stage],
            recv_sem=rs_recv.at[stage],
            device_id={"box": partner},
            device_id_type=MESH,
        )

        def finish(last):
            copy.wait()
            target = far if last else buf
            target[pl.ds(keep, size)] = buf[pl.ds(keep, size)] + landed[pl.ds(spot, size)]

        return copy, finish

    def doubling(stage):
        size = rows >> (stage + 1)
        low = 0
        for s in range(stage + 1):
            low = low + (me // (1 << s) % 2) * (rows >> (s + 1))
        bit = me // (1 << stage) % 2
        partner = me + (1 - 2 * bit) * (1 << stage)
        return pltpu.make_async_remote_copy(
            src_ref=far.at[pl.ds(low, size)],
            dst_ref=far.at[pl.ds(low, size)],
            send_sem=ag_send.at[stage],
            recv_sem=ag_recv.at[stage],
            device_id={"box": partner},
            device_id_type=MESH,
        )

    copies = [None] * stages
    copies[0] = halving(0)
    copies[0][0].start()

    tile = 256
    for parent_at in range(groups8):

        def lift(t, carry, parent_at=parent_at):
            at = pl.multiple_of(t * tile, tile)
            left = lift_ref[pl.ds(at, tile), :]
            real = jnp.zeros((tile, illums), F32)
            imag = jnp.zeros((tile, illums), F32)
            for child in range(8):
                b = parent_at * 8 + child
                both = dot(left, jnp.concatenate([pat_ref[0, b], pat_ref[1, b]], axis=1))
                cosine = phase_ref[pl.ds(at, tile), child : child + 1]
                sine = phase_ref[pl.ds(at, tile), 8 + child : 9 + child]
                re, im = both[:, :illums], both[:, illums:]
                real = real + (cosine * re - sine * im)
                imag = imag + (cosine * im + sine * re)
            parent[parent_at, pl.ds(at, tile), :] = real.astype(BF16)
            parent[groups8 + parent_at, pl.ds(at, tile), :] = imag.astype(BF16)
            return carry

        lax.fori_loop(0, qdir // tile, lift, 0)

    def out_copy(i):
        peer = lax.rem(me + i, n)
        return pltpu.make_async_remote_copy(
            src_ref=parent.at[:, pl.ds(pl.multiple_of(peer * qloc, qloc), qloc), :],
            dst_ref=arrived.at[me],
            send_sem=out_send.at[i],
            recv_sem=out_recv.at[i],
            device_id={"box": peer},
            device_id_type=MESH,
        )

    def start_out(i, carry):
        out_copy(i).start()
        return carry

    lax.fori_loop(1, n, start_out, 0)

    copies[0][1](stages == 1)
    if stages > 1:
        copies[1] = halving(1)
        copies[1][0].start()

    for part in range(2):
        for b in range(boxes):
            own_wide[pl.ds((part * boxes + b) * kdir, kdir), :] = pat_ref[part, b].astype(F32)
    unroll = 4

    def near_own(t, carry):
        for u in range(unroll):
            k = t * unroll + u
            sources = own_wide[pl.ds(k, 2 * boxes, stride=kdir), :].astype(BF16)
            acc[pl.ds(k, 2 * boxes, stride=kdir), :] = dot(own_op_ref[k], sources)
        return carry

    lax.fori_loop(0, kdir // unroll, near_own, 0)

    def widen(source, value):
        for part in range(2):
            for p in range(groups8):
                s = (part * n + source) * groups8 + p
                at = pl.multiple_of(s * qloc, qloc)
                wide[pl.ds(at, qloc), :] = value(part * groups8 + p).astype(F32)

    widen(me, lambda c: parent[c, pl.ds(pl.multiple_of(me * qloc, qloc), qloc), :])

    def take(i, carry):
        out_copy(i).wait()
        source = lax.rem(me - i + n, n)
        widen(source, lambda c: arrived[source, c])
        return carry

    lax.fori_loop(1, n, take, 0)
    parents2 = 2 * n * groups8

    def translate(t, carry):
        for u in range(unroll):
            q = t * unroll + u
            sources = wide[pl.ds(q, parents2, stride=qloc), :].astype(BF16)
            result[pl.ds(q, parents2, stride=qloc), :] = dot(couple_ref[q], sources)
        return carry

    lax.fori_loop(0, qloc // unroll, translate, 0)
    result_send[...] = result[...].reshape(2, n * groups8, qloc, illums).astype(BF16)

    def back_copy(i):
        peer = lax.rem(me + i, n)
        return pltpu.make_async_remote_copy(
            src_ref=result_send.at[:, pl.ds(peer * groups8, groups8)],
            dst_ref=returned.at[:, :, pl.ds(pl.multiple_of(me * qloc, qloc), qloc), :],
            send_sem=back_send.at[i],
            recv_sem=back_recv.at[i],
            device_id={"box": peer},
            device_id_type=MESH,
        )

    def start_back(i, carry):
        back_copy(i).start()
        return carry

    lax.fori_loop(1, n, start_back, 0)
    returned[:, :, pl.ds(pl.multiple_of(me * qloc, qloc), qloc), :] = result_send[:, pl.ds(me * groups8, groups8)]

    for stage in range(1, stages):
        copies[stage][1](stage == stages - 1)
        if stage + 1 < stages:
            copies[stage + 1] = halving(stage + 1)
            copies[stage + 1][0].start()
    for stage in reversed(range(stages)):
        copy = doubling(stage)
        copy.start()
        copy.wait()

    def widen_far(j, carry):
        far_wide[pl.ds(pl.multiple_of(j * kdir, kdir), kdir), :] = far[j].astype(F32)
        return carry

    lax.fori_loop(0, rows, widen_far, 0)

    def near_far(t, carry):
        for u in range(unroll):
            k = t * unroll + u
            sources = far_wide[pl.ds(k, rows, stride=kdir), :].astype(BF16)
            spots = pl.ds(k, 2 * boxes, stride=kdir)
            acc[spots, :] = acc[spots, :] + dot(far_op_ref[k], sources)
        return carry

    lax.fori_loop(0, kdir // unroll, near_far, 0)

    def land(i, carry):
        back_copy(i).wait()
        return carry

    lax.fori_loop(1, n, land, 0)

    for parent_at in range(groups8):
        for child in range(8):
            b = parent_at * 8 + child
            re = returned[0, parent_at].astype(F32)
            im = returned[1, parent_at].astype(F32)
            cosine = phase_ref[:, child : child + 1]
            sine = phase_ref[:, 8 + child : 9 + child]
            real = (cosine * re + sine * im).astype(BF16)
            imag = (cosine * im - sine * re).astype(BF16)
            both = dot(interp_ref[...], jnp.concatenate([real, imag], axis=1))
            out_ref[0, b] = acc[pl.ds(b * kdir, kdir), :] + both[:, :illums]
            out_ref[1, b] = acc[pl.ds((boxes + b) * kdir, kdir), :] + both[:, illums:]


def block_complex(real, imag):
    top = jnp.concatenate([real, -imag], axis=2)
    bottom = jnp.concatenate([imag, real], axis=2)
    return jnp.concatenate([top, bottom], axis=1)


def shards(
    patterns,
    owner_block,
    low_index,
    low_mask,
    low_table,
    interp,
    shift_angle,
    par_source,
    par_index,
    par_mask,
    par_table,
):
    boxes, kdir, illums = patterns.shape[1:]
    groups8 = boxes // 8
    qdir = interp.shape[1]
    n = lax.axis_size("box")
    listed = owner_block.shape[0]
    parents = par_source.shape[0]
    qloc = qdir // n
    rows = 2 * listed * 8
    sources = low_index.shape[1]

    ntrans = low_table.shape[1]
    kinds = jnp.arange(ntrans, dtype=jnp.int32)
    low_code = jnp.where(low_mask > 0, low_index, -1)
    low_hot = (low_code[:, :, None] == kinds).astype(BF16).reshape(boxes * sources, ntrans)
    low_op = jnp.einsum("ctk,nt->ckn", low_table, low_hot, preferred_element_type=F32)
    low_op = low_op.astype(BF16).reshape(2, kdir, boxes, sources)
    own_op = block_complex(low_op[0, :, :, :boxes], low_op[1, :, :, :boxes])
    far_op = block_complex(low_op[0, :, :, boxes:], low_op[1, :, :, boxes:])

    start = lax.axis_index("box") * qloc
    table = lax.dynamic_slice_in_dim(par_table, start, qloc, 2)
    match = par_source[:, :, None] == jnp.arange(parents, dtype=jnp.int32)
    match = match & (par_mask[:, :, None] > 0)
    par_code = jnp.sum(jnp.where(match, par_index[:, :, None] + 1, 0), axis=1) - 1
    par_kinds = jnp.arange(par_table.shape[1], dtype=jnp.int32)
    par_hot = (par_code[:, :, None] == par_kinds).astype(BF16).reshape(parents * parents, -1)
    couple = jnp.einsum("ctq,nt->cqn", table, par_hot, preferred_element_type=F32)
    couple = couple.astype(BF16).reshape(2, qloc, parents, parents)
    couple = block_complex(couple[0], couple[1])

    phase = jnp.concatenate([jnp.cos(shift_angle), jnp.sin(shift_angle)], axis=0).T

    vmem = pl.BlockSpec(memory_space=pltpu.VMEM)
    smem = pl.BlockSpec(memory_space=pltpu.SMEM)
    stages = n.bit_length() - 1
    dma = pltpu.SemaphoreType.DMA
    return pl.pallas_call(
        functools.partial(kernel, n, listed),
        out_shape=jax.ShapeDtypeStruct((2, boxes, kdir, illums), F32),
        in_specs=[smem] + [vmem] * 7,
        out_specs=vmem,
        scratch_shapes=[
            pltpu.VMEM((2 * groups8, qdir, illums), BF16),
            pltpu.VMEM((n, 2 * groups8, qloc, illums), BF16),
            pltpu.VMEM((2 * parents * qloc, illums), F32),
            pltpu.VMEM((2 * parents * qloc, illums), F32),
            pltpu.VMEM((2, parents, qloc, illums), BF16),
            pltpu.VMEM((2, groups8, qdir, illums), BF16),
            pltpu.VMEM((rows, kdir, illums), BF16),
            pltpu.VMEM((rows, kdir, illums), BF16),
            pltpu.VMEM((rows, kdir, illums), BF16),
            pltpu.VMEM((rows * kdir, illums), F32),
            pltpu.VMEM((2 * boxes * kdir, illums), F32),
            pltpu.VMEM((2 * boxes * kdir, illums), F32),
            dma((n,)),
            dma((n,)),
            dma((n,)),
            dma((n,)),
            dma((stages,)),
            dma((stages,)),
            dma((stages,)),
            dma((stages,)),
        ],
        compiler_params=pltpu.CompilerParams(
            collective_id=0, has_side_effects=True, vmem_limit_bytes=56 * 1024 * 1024
        ),
    )(owner_block, patterns, own_op, far_op, interp, interp.T, phase, couple)


def solution(mesh):
    placed = (
        P(None, "box", None, "illum"),
        P(),
        P("box", None),
        P("box", None),
        P(),
        P(),
        P(),
        P(),
        P(),
        P(),
        P(),
    )
    return jax.shard_map(
        shards, mesh=mesh, in_specs=placed, out_specs=P(None, "box", None, "illum"), check_vma=False
    )
```

time: 169 us -> 107 us (0.63)
  Pallas kernels: 0 us -> 88.6 us
  waiting for transfers between devices: 81.4 us -> 0 us
  between operations: 24.5 us -> 0.15 us
  matrix products: 16.7 us -> 0.88 us
  starting transfers between devices: 13.5 us -> 0 us
  local copies, waits for them, and re-layouts: 21.9 us -> 11.4 us
  other arithmetic: 10.9 us -> 5.28 us
    pallas_call x0 -> x1, Pallas kernels: none -> 88.6 us  [shards(): pl.pallas_call(functools.partial(kernel, n, listed), out_shape=jax.ShapeD...]
    psum x1 -> x0, waiting for transfers between devices: 81.3 us -> none  [broadcast(): return lax.psum(jnp.where(mine, x, jnp.zeros_like(x)), axis)]
    dot_general x15 -> x2, matrix products: 16.7 us -> 0.88 us  [the longest x1 0.51 us: shards(): jnp.einsum('ctk,nt->ckn', low_table, low_hot, preferred_element_type=F32)]
    all_to_all x2 -> x0, starting transfers between devices: 13.4 us -> none  [the longest x1 7.41 us: shards(): lax.all_to_all(parent_local, 'box', split_axis=2, concat_axis=1, tiled=True)]
    gather x3 -> x0, local copies, waits for them, and re-layouts: 6.44 us -> none  [the longest x2 4.33 us: shards(): low_table[:, low_index] * low_mask[None, :, :, None].astype(jnp.bfloat16)]
    unnamed x30 -> x9, local copies, waits for them, and re-layouts: 3.18 us -> 6.47 us
    concatenate x1 -> x2, local copies, waits for them, and re-layouts: 0.13 us -> 3.13 us  [the longest x1 2.3 us: block_complex(): return jnp.concatenate([top, bottom], axis=1)]
    concatenate x0 -> x4, other arithmetic: none -> 2.67 us  [the longest x3 2.67 us: block_complex(): return jnp.concatenate([top, bottom], axis=1)]
  transfers between devices with their start and end apart: 3 -> 0, of which waited for: 1 -> 0; matrix products, arithmetic and copies ran while one was open for 17% -> 0% of each run, Pallas kernels for 0% -> 0%
where the time goes in v1:
time: 107 us; the launch traced here: 106 us
  Pallas kernels  88.6 us (83%)
  local copies, waits for them, and re-layouts  11.4 us (11%)
  other arithmetic  5.28 us (5%)
    pallas_call x1, Pallas kernels, shards(): pl.pallas_call(functools.partial(kernel, n, listed), out_shape=jax.ShapeD...  88.6 us
    unnamed x9, local copies, waits for them, and re-layouts  6.47 us
    concatenate x3, other arithmetic, block_complex(): return jnp.concatenate([top, bottom], axis=1)  2.67 us
    concatenate x1, local copies, waits for them, and re-layouts, block_complex(): return jnp.concatenate([top, bottom], axis=1)  2.3 us

profile of v1, /device:TPU:0, one launch (start us, length us, event | category | flops | bytes accessed | tf_op | source)
XLA Modules:
  0.0 106.3 jit_solution(6379209225019945023)
XLA Ops:
  0.0 0.8 broadcast_compare_fusion
  0.8 0.1 copy.50
  0.9 0.7 compare_select_fusion
  1.6 0.1 eq.43
  1.7 0.7 broadcast_add_fusion.1
  2.4 0.1 copy.51
  2.4 0.8 copy.49
  3.2 0.3 select_reduce_fusion
  3.5 0.1 sub.7
  3.6 0.8 fusion.16
  4.4 1.7 %copy.46 = bf16[128,512]{0,1:T(8,128)(2,1)} copy(bf16[128,512]{1,0:T(8,128)(2,1)} %interp_ref.1) | data formatting | bytes 262144 | tf_op args[5]
  6.1 0.2 constant_dynamic-slice_fusion
  6.3 0.4 fusion.3
  6.7 0.2 squeeze.23
  6.9 0.8 copy.47
  7.8 0.2 squeeze.22
  8.0 1.1 %maximum_maximum_fusion.1.couple_ref = bf16[32,64,64]{2,1,0:T(8,128)(2,1)} fusion(bf16[32,32,32]{2,1,0:T(8,128)(2,1)S(1)} %squeeze.22, bf16[32,32,32]{2,1,0:T(8,128)(2,1)S(1)} %squeeze.23, bf16[32,32,32]{2,1,0:T(8,128)(2,1)S(1)} %neg.11), kind=kLoop, calls=%fused_computation.9 | loop fusion | flops 1048576 | bytes 458752 | tf_op jit(solution)/shard_map/concatenate | solution.py:279
  9.1 0.5 convolution_convert_fusion
  9.7 0.4 copy.54
  10.2 0.4 copy.53
  10.7 1.6 %maximum_maximum_fusion.far_op_ref = bf16[128,32,64]{2,1,0:T(8,128)(2,1)} fusion(bf16[128,16,32]{2,1,0:T(8,128)(2,1)S(1)} %bitcast.23, bf16[128,16,32]{2,1,0:T(8,128)(2,1)S(1)} %bitcast.22, bf16[128,16,32]{2,1,0:T(8,128)(2,1)S(1)} %bitcast_negate_fusion), kind=kLoop, calls=%fused_computation.5 | loop fusion | flops 2097152 | bytes 917504 | tf_op jit(solution)/shard_map/concatenate | solution.py:279
  12.2 2.3 %copy.52.own_op_ref = bf16[128,32,32]{2,1,0:T(8,128)(2,1)} copy(bf16[128,32,32]{0,2,1:T(8,128)(2,1)S(1)} %maximum_maximum_fusion.2) | data formatting | bytes 524288 | tf_op jit(solution)/shard_map/concatenate | solution.py:279
  14.5 88.6 %shard_map.109 = f32[2,16,128,128]{3,2,1,0:T(8,128)} custom-call(s32[4]{0:T(128)} %owner_ref.1, bf16[2,16,128,128]{3,2,1,0:T(8,128)(2,1)} %pat_ref.1, bf16[128,32,32]{2,1,0:T(8,128)(2,1)} %copy.52.own_op_ref, bf16[128,32,64]{2,1,0:T(8,128)(2,1)} %maximum_maximum_fusion.far_op_ref, bf16[128,512]{1,0:T(8,128)(2,1)} %interp_ref.1, bf16[512,128]{1,0:T(8,128)(2,1)} %bitcast.28, ...), custom_call_target="tpu_custom_call" | custom-call | tf_op jit(solution)/shard_map/pallas_call | solution.py:331
  103.1 3.1 %copy.61 = f32[2,16,128,128]{3,2,1,0:T(8,128)} copy(f32[2,16,128,128]{3,2,1,0:T(8,128)} %shard_map.109) | data formatting | bytes 4194304
  (13 shorter events, 0.2 us)
Async XLA Ops:
  0.0 6.1 %copy-start = (bf16[2,316,512]{2,0,1:T(2,128)(2,1)S(1)}, bf16[2,316,512]{2,0,1:T(2,128)(2,1)}, u32[]{:S(2)}) copy-start(bf16[2,316,512]{2,0,1:T(2,128)(2,1)} %param.21) | copy-start | bytes 1941508
  4.4 4.7 %copy-start.1 = (bf16[2,316,128]{2,0,1:T(2,128)(2,1)S(1)}, bf16[2,316,128]{2,0,1:T(2,128)(2,1)}, u32[]{:S(2)}) copy-start(bf16[2,316,128]{2,0,1:T(2,128)(2,1)} %param.15) | copy-start | bytes 485380

commit v2 on v1

--- a/solution.py
+++ b/solution.py
@@ -39,7 +39,6 @@
     far,
     far_wide,
     own_wide,
-    acc,
     out_send,
     out_recv,
     back_send,
@@ -77,51 +76,72 @@
 
     pl.semaphore_wait(barrier, n - 1)
 
-    def halving(stage):
-        size = rows >> (stage + 1)
-        low = 0
-        for s in range(stage):
-            low = low + (me // (1 << s) % 2) * (rows >> (s + 1))
-        bit = me // (1 << stage) % 2
-        keep = low + bit * size
-        give = low + (1 - bit) * size
-        partner = me + (1 - 2 * bit) * (1 << stage)
-        spot = rows - 2 * size
-        copy = pltpu.make_async_remote_copy(
-            src_ref=buf.at[pl.ds(give, size)],
-            dst_ref=landed.at[pl.ds(spot, size)],
-            send_sem=rs_send.at[stage],
-            recv_sem=rs_recv.at[stage],
-            device_id={"box": partner},
+    half = rows // 2
+    later = list(range(1, stages))
+    cut = (stages + 1) // 2
+    chains = [later, [b for b in later if b >= cut] + [b for b in later if b < cut]]
+
+    def place(chain, depth):
+        low = me % 2 * half + chain * (half // 2)
+        size = half // 2
+        for b in chains[chain][:depth]:
+            size = size // 2
+            low = low + me // (1 << b) % 2 * size
+        return low, size
+
+    def remote(src, dst, send, recv, bit):
+        mine = me // (1 << bit) % 2
+        return pltpu.make_async_remote_copy(
+            src_ref=src,
+            dst_ref=dst,
+            send_sem=send,
+            recv_sem=recv,
+            device_id={"box": me + (1 - 2 * mine) * (1 << bit)},
             device_id_type=MESH,
         )
 
-        def finish(last):
-            copy.wait()
-            target = far if last else buf
-            target[pl.ds(keep, size)] = buf[pl.ds(keep, size)] + landed[pl.ds(spot, size)]
-
-        return copy, finish
-
-    def doubling(stage):
-        size = rows >> (stage + 1)
-        low = 0
-        for s in range(stage + 1):
-            low = low + (me // (1 << s) % 2) * (rows >> (s + 1))
-        bit = me // (1 << stage) % 2
-        partner = me + (1 - 2 * bit) * (1 << stage)
-        return pltpu.make_async_remote_copy(
-            src_ref=far.at[pl.ds(low, size)],
-            dst_ref=far.at[pl.ds(low, size)],
-            send_sem=ag_send.at[stage],
-            recv_sem=ag_recv.at[stage],
-            device_id={"box": partner},
-            device_id_type=MESH,
+    def first_swap():
+        give = (1 - me % 2) * half
+        return remote(
+            buf.at[pl.ds(give, half)], landed.at[pl.ds(0, half)], rs_send.at[0, 0], rs_recv.at[0, 0], 0
         )
 
-    copies = [None] * stages
-    copies[0] = halving(0)
-    copies[0][0].start()
+    def halving(chain, depth):
+        bit = chains[chain][depth]
+        low, size = place(chain, depth)
+        size = size // 2
+        give = low + (1 - me // (1 << bit) % 2) * size
+        spot = half + chain * (half // 2) + half // 2 - 2 * size
+        return remote(
+            buf.at[pl.ds(give, size)],
+            landed.at[pl.ds(spot, size)],
+            rs_send.at[chain, 1 + depth],
+            rs_recv.at[chain, 1 + depth],
+            bit,
+        )
+
+    def halve(chain, depth):
+        halving(chain, depth).wait()
+        low, size = place(chain, depth + 1)
+        spot = half + chain * (half // 2) + half // 2 - 2 * size
+        target = far if depth + 1 == len(later) else buf
+        target[pl.ds(low, size)] = buf[pl.ds(low, size)] + landed[pl.ds(spot, size)]
+        if depth + 1 < len(later):
+            halving(chain, depth + 1).start()
+        else:
+            doubling(chain, len(later)).start()
+
+    def doubling(chain, depth):
+        low, size = place(chain, depth)
+        bit = chains[chain][depth - 1] if depth else 0
+        spots = far.at[pl.ds(low, size)]
+        return remote(spots, spots, ag_send.at[chain, depth], ag_recv.at[chain, depth], bit)
+
+    def double(chain, depth):
+        doubling(chain, depth).wait()
+        doubling(chain, depth - 1).start()
+
+    first_swap().start()
 
     tile = 256
     for parent_at in range(groups8):
@@ -162,10 +182,11 @@
 
     lax.fori_loop(1, n, start_out, 0)
 
-    copies[0][1](stages == 1)
-    if stages > 1:
-        copies[1] = halving(1)
-        copies[1][0].start()
+    first_swap().wait()
+    kept = pl.ds(me % 2 * half, half)
+    buf[kept] = buf[kept] + landed[pl.ds(0, half)]
+    halving(0, 0).start()
+    halving(1, 0).start()
 
     for part in range(2):
         for b in range(boxes):
@@ -176,10 +197,13 @@
         for u in range(unroll):
             k = t * unroll + u
             sources = own_wide[pl.ds(k, 2 * boxes, stride=kdir), :].astype(BF16)
-            acc[pl.ds(k, 2 * boxes, stride=kdir), :] = dot(own_op_ref[k], sources)
+            out_ref[pl.ds(k, 2 * boxes, stride=kdir), :] = dot(own_op_ref[k], sources)
         return carry
 
     lax.fori_loop(0, kdir // unroll, near_own, 0)
+
+    for chain in range(2):
+        halve(chain, 0)
 
     def widen(source, value):
         for part in range(2):
@@ -227,31 +251,12 @@
     lax.fori_loop(1, n, start_back, 0)
     returned[:, :, pl.ds(pl.multiple_of(me * qloc, qloc), qloc), :] = result_send[:, pl.ds(me * groups8, groups8)]
 
-    for stage in range(1, stages):
-        copies[stage][1](stage == stages - 1)
-        if stage + 1 < stages:
-            copies[stage + 1] = halving(stage + 1)
-            copies[stage + 1][0].start()
-    for stage in reversed(range(stages)):
-        copy = doubling(stage)
-        copy.start()
-        copy.wait()
-
-    def widen_far(j, carry):
-        far_wide[pl.ds(pl.multiple_of(j * kdir, kdir), kdir), :] = far[j].astype(F32)
-        return carry
-
-    lax.fori_loop(0, rows, widen_far, 0)
-
-    def near_far(t, carry):
-        for u in range(unroll):
-            k = t * unroll + u
-            sources = far_wide[pl.ds(k, rows, stride=kdir), :].astype(BF16)
-            spots = pl.ds(k, 2 * boxes, stride=kdir)
-            acc[spots, :] = acc[spots, :] + dot(far_op_ref[k], sources)
-        return carry
-
-    lax.fori_loop(0, kdir // unroll, near_far, 0)
+    for depth in range(1, len(later)):
+        for chain in range(2):
+            halve(chain, depth)
+    for depth in range(len(later), 1, -1):
+        for chain in range(2):
+            double(chain, depth)
 
     def land(i, carry):
         back_copy(i).wait()
@@ -269,8 +274,35 @@
             real = (cosine * re + sine * im).astype(BF16)
             imag = (cosine * im - sine * re).astype(BF16)
             both = dot(interp_ref[...], jnp.concatenate([real, imag], axis=1))
-            out_ref[0, b] = acc[pl.ds(b * kdir, kdir), :] + both[:, :illums]
-            out_ref[1, b] = acc[pl.ds((boxes + b) * kdir, kdir), :] + both[:, illums:]
+            spots = pl.ds(b * kdir, kdir)
+            out_ref[spots, :] = out_ref[spots, :] + both[:, :illums]
+            spots = pl.ds((boxes + b) * kdir, kdir)
+            out_ref[spots, :] = out_ref[spots, :] + both[:, illums:]
+
+    for chain in range(2):
+        double(chain, 1)
+
+    def near_half(part):
+        def widen_far(j, carry):
+            far_wide[pl.ds(pl.multiple_of(j * kdir, kdir), kdir), :] = far[part * half + j].astype(F32)
+            return carry
+
+        lax.fori_loop(0, half, widen_far, 0)
+
+        def near_far(t, carry):
+            for u in range(unroll):
+                k = t * unroll + u
+                sources = far_wide[pl.ds(k, half, stride=kdir), :].astype(BF16)
+                spots = pl.ds(k, 2 * boxes, stride=kdir)
+                out_ref[spots, :] = out_ref[spots, :] + dot(far_op_ref[part, k], sources)
+            return carry
+
+        lax.fori_loop(0, kdir // unroll, near_far, 0)
+
+    near_half(me % 2)
+    for chain in range(2):
+        doubling(chain, 0).wait()
+    near_half(1 - me % 2)
 
 
 def block_complex(real, imag):
@@ -309,7 +341,13 @@
     low_op = jnp.einsum("ctk,nt->ckn", low_table, low_hot, preferred_element_type=F32)
     low_op = low_op.astype(BF16).reshape(2, kdir, boxes, sources)
     own_op = block_complex(low_op[0, :, :, :boxes], low_op[1, :, :, :boxes])
-    far_op = block_complex(low_op[0, :, :, boxes:], low_op[1, :, :, boxes:])
+    far_real, far_imag = low_op[0, :, :, boxes:], low_op[1, :, :, boxes:]
+    far_op = jnp.stack(
+        [
+            jnp.concatenate([far_real, far_imag], axis=1),
+            jnp.concatenate([-far_imag, far_real], axis=1),
+        ]
+    )
 
     start = lax.axis_index("box") * qloc
     table = lax.dynamic_slice_in_dim(par_table, start, qloc, 2)
@@ -330,7 +368,7 @@
     dma = pltpu.SemaphoreType.DMA
     return pl.pallas_call(
         functools.partial(kernel, n, listed),
-        out_shape=jax.ShapeDtypeStruct((2, boxes, kdir, illums), F32),
+        out_shape=jax.ShapeDtypeStruct((2 * boxes * kdir, illums), F32),
         in_specs=[smem] + [vmem] * 7,
         out_specs=vmem,
         scratch_shapes=[
@@ -343,22 +381,21 @@
             pltpu.VMEM((rows, kdir, illums), BF16),
             pltpu.VMEM((rows, kdir, illums), BF16),
             pltpu.VMEM((rows, kdir, illums), BF16),
-            pltpu.VMEM((rows * kdir, illums), F32),
-            pltpu.VMEM((2 * boxes * kdir, illums), F32),
+            pltpu.VMEM((rows // 2 * kdir, illums), F32),
             pltpu.VMEM((2 * boxes * kdir, illums), F32),
             dma((n,)),
             dma((n,)),
             dma((n,)),
             dma((n,)),
-            dma((stages,)),
-            dma((stages,)),
-            dma((stages,)),
-            dma((stages,)),
+            dma((2, stages)),
+            dma((2, stages)),
+            dma((2, stages)),
+            dma((2, stages)),
         ],
         compiler_params=pltpu.CompilerParams(
             collective_id=0, has_side_effects=True, vmem_limit_bytes=56 * 1024 * 1024
         ),
-    )(owner_block, patterns, own_op, far_op, interp, interp.T, phase, couple)
+    )(owner_block, patterns, own_op, far_op, interp, interp.T, phase, couple).reshape(2, boxes, kdir, illums)
 
 
 def solution(mesh):

time: 107 us -> 101 us (0.944)
  Pallas kernels: 88.6 us -> 81.6 us
  local copies, waits for them, and re-layouts: 11.4 us -> 14.2 us
  other arithmetic: 5.28 us -> 3.75 us
    pallas_call x1, Pallas kernels: 88.6 us -> 81.6 us  [shards(): pl.pallas_call(functools.partial(kernel, n, listed), out_shape=jax.ShapeD...]
    another operation x0 -> x1, local copies, waits for them, and re-layouts: none -> 3.65 us  [shards(): jnp.stack([jnp.concatenate([far_real, far_imag], axis=1), jnp.concatenate...]
    concatenate x3 -> x2, other arithmetic: 2.67 us -> 1.09 us  [block_complex(): return jnp.concatenate([top, bottom], axis=1)]
    unnamed x9 -> x7, local copies, waits for them, and re-layouts: 6.47 us -> 5.63 us
where the time goes in v2:
time: 101 us
  Pallas kernels  81.6 us (81%)
  local copies, waits for them, and re-layouts  14.2 us (14%)
  other arithmetic  3.75 us (4%)
    pallas_call x1, Pallas kernels, shards(): pl.pallas_call(functools.partial(kernel, n, listed), out_shape=jax.ShapeD...  81.6 us
    unnamed x7, local copies, waits for them, and re-layouts  5.63 us
    another operation x1, local copies, waits for them, and re-layouts, shards(): jnp.stack([jnp.concatenate([far_real, far_imag], axis=1), jnp.concatenate...  3.65 us
    concatenate x1, local copies, waits for them, and re-layouts, block_complex(): return jnp.concatenate([top, bottom], axis=1)  2.32 us

profile of v2, /device:TPU:0, one launch (start us, length us, event | category | flops | bytes accessed | tf_op | source)
XLA Modules:
  0.0 100.5 jit_solution(336596553539820877)
XLA Ops:
  0.0 0.8 broadcast_compare_fusion
  0.8 0.1 copy.47
  0.9 0.7 compare_select_fusion
  1.6 0.1 eq.43
  1.7 0.7 broadcast_add_fusion.1
  2.4 0.1 copy.48
  2.4 0.8 copy.46
  3.2 0.3 select_reduce_fusion
  3.5 0.1 sub.7
  3.6 0.8 fusion.16
  4.4 1.7 %copy.43 = bf16[128,512]{0,1:T(8,128)(2,1)} copy(bf16[128,512]{1,0:T(8,128)(2,1)} %interp_ref.1) | data formatting | bytes 262144 | tf_op args[5]
  6.1 0.2 constant_dynamic-slice_fusion
  6.4 0.4 fusion.3
  6.8 0.2 squeeze.23
  7.0 0.8 copy.44
  7.8 0.1 neg.11
  7.8 0.2 squeeze.22
  8.0 1.1 %maximum_maximum_fusion.couple_ref = bf16[32,64,64]{2,1,0:T(8,128)(2,1)} fusion(bf16[32,32,32]{2,1,0:T(8,128)(2,1)S(1)} %squeeze.22, bf16[32,32,32]{2,1,0:T(8,128)(2,1)S(1)} %squeeze.23, bf16[32,32,32]{2,1,0:T(8,128)(2,1)S(1)} %neg.11), kind=kLoop, calls=%fused_computation.9 | loop fusion | flops 1048576 | bytes 458752 | tf_op jit(solution)/shard_map/concatenate | solution.py:311
  9.1 0.5 convolution_convert_fusion
  9.8 0.1 pad_maximum_fusion
  9.9 2.3 %copy.49.own_op_ref = bf16[128,32,32]{2,1,0:T(8,128)(2,1)} copy(bf16[128,32,32]{0,2,1:T(8,128)(2,1)S(1)} %maximum_maximum_fusion.1) | data formatting | bytes 524288 | tf_op jit(solution)/shard_map/concatenate | solution.py:311
  12.2 3.6 %copy.50.far_op_ref = bf16[2,128,32,32]{3,2,1,0:T(8,128)(2,1)} copy(bf16[2,128,32,32]{1,3,2,0:T(8,128)(2,1)S(1)} %pad_maximum_fusion) | data formatting | bytes 1048576 | tf_op jit(solution)/shard_map/stack | solution.py:345
  15.8 81.6 %shard_map.109 = f32[4096,128]{1,0:T(8,128)} custom-call(s32[4]{0:T(128)} %owner_ref.1, bf16[2,16,128,128]{3,2,1,0:T(8,128)(2,1)} %pat_ref.1, bf16[128,32,32]{2,1,0:T(8,128)(2,1)} %copy.49.own_op_ref, bf16[2,128,32,32]{3,2,1,0:T(8,128)(2,1)} %copy.50.far_op_ref, bf16[128,512]{1,0:T(8,128)(2,1)} %interp_ref.1, bf16[512,128]{1,0:T(8,128)(2,1)} %bitcast.36, ...), custom_call_target="tpu_custom_call" | custom-call | tf_op jit(solution)/shard_map/pallas_call | solution.py:369
  97.4 3.1 %copy.57 = f32[2,16,128,128]{3,2,1,0:T(8,128)} copy(f32[2,16,128,128]{3,2,1,0:T(8,128)} %bitcast.30) | data formatting | bytes 4194304
  (13 shorter events, 0.2 us)
Async XLA Ops:
  0.0 6.1 %copy-start = (bf16[2,316,512]{2,0,1:T(2,128)(2,1)S(1)}, bf16[2,316,512]{2,0,1:T(2,128)(2,1)}, u32[]{:S(2)}) copy-start(bf16[2,316,512]{2,0,1:T(2,128)(2,1)} %param.21) | copy-start | bytes 1941508
  4.4 4.7 %copy-start.1 = (bf16[2,316,128]{2,0,1:T(2,128)(2,1)S(1)}, bf16[2,316,128]{2,0,1:T(2,128)(2,1)}, u32[]{:S(2)}) copy-start(bf16[2,316,128]{2,0,1:T(2,128)(2,1)} %param.15) | copy-start | bytes 485380

commit v3 on v2

--- a/solution.py
+++ b/solution.py
@@ -21,13 +21,17 @@
     listed,
     owner_ref,
     pat_ref,
-    own_op_ref,
-    far_op_ref,
+    code_ref,
+    table_ref,
+    source_ref,
+    index_ref,
+    mask_ref,
+    par_ref,
     interp_ref,
-    lift_ref,
     phase_ref,
-    couple_ref,
     out_ref,
+    op,
+    couple,
     parent,
     arrived,
     wide,
@@ -52,7 +56,7 @@
     boxes = pat_ref.shape[1]
     kdir, illums = pat_ref.shape[2], pat_ref.shape[3]
     groups8 = boxes // 8
-    qdir = lift_ref.shape[0]
+    qdir = interp_ref.shape[1]
     qloc = qdir // n
     rows = 2 * listed * 8
     stages = n.bit_length() - 1
@@ -148,7 +152,7 @@
 
         def lift(t, carry, parent_at=parent_at):
             at = pl.multiple_of(t * tile, tile)
-            left = lift_ref[pl.ds(at, tile), :]
+            left = interp_ref[:, pl.ds(at, tile)].T
             real = jnp.zeros((tile, illums), F32)
             imag = jnp.zeros((tile, illums), F32)
             for child in range(8):
@@ -188,19 +192,49 @@
     halving(0, 0).start()
     halving(1, 0).start()
 
-    for part in range(2):
-        for b in range(boxes):
-            own_wide[pl.ds((part * boxes + b) * kdir, kdir), :] = pat_ref[part, b].astype(F32)
     unroll = 4
-
-    def near_own(t, carry):
-        for u in range(unroll):
-            k = t * unroll + u
-            sources = own_wide[pl.ds(k, 2 * boxes, stride=kdir), :].astype(BF16)
-            out_ref[pl.ds(k, 2 * boxes, stride=kdir), :] = dot(own_op_ref[k], sources)
-        return carry
-
-    lax.fori_loop(0, kdir // unroll, near_own, 0)
+    parents = n * groups8
+    parents2 = 2 * parents
+
+    lanes = lax.broadcasted_iota(jnp.int32, (parents, parents), 1)
+    code = jnp.zeros((parents, parents), jnp.int32)
+    slot_code = jnp.where(mask_ref[...] > 0, index_ref[...] + 1, 0)
+    for j in range(source_ref.shape[1]):
+        code = code + jnp.where(source_ref[:, j : j + 1] == lanes, slot_code[:, j : j + 1], 0)
+    code = jnp.concatenate([code, code], axis=1) - 1
+    each = max(1, 256 // parents2)
+    kinds = lax.broadcasted_iota(jnp.int32, (par_ref.shape[1], each * parents2), 0)
+    first = lax.broadcasted_iota(jnp.int32, (qloc, parents2), 1) < parents
+    for p in range(0, parents, each):
+        row = jnp.concatenate([code[p + u : p + u + 1] for u in range(each)], axis=1)
+        hot = jnp.where(kinds == row, 1.0, 0.0).astype(BF16)
+        got = dot(par_ref[...], hot)
+        for u in range(each):
+            real = got[:qloc, u * parents2 : (u + 1) * parents2]
+            imag = got[qloc:, u * parents2 : (u + 1) * parents2]
+            couple[pl.ds(p + u, qloc, stride=parents2), :] = jnp.where(first, real, -imag)
+            couple[pl.ds(parents + p + u, qloc, stride=parents2), :] = jnp.where(first, imag, real)
+
+    width = code_ref.shape[1]
+    low_kinds = lax.broadcasted_iota(jnp.int32, (table_ref.shape[1], 2 * width), 0)
+    lane = lax.broadcasted_iota(jnp.int32, (kdir, width), 1)
+    flip = me % 2
+    column = jnp.where(
+        lane < 2 * boxes, lane // boxes, jnp.where(lane < 2 * boxes + half, flip, 1 - flip)
+    )
+    low_first = column == 0
+    for b in range(0, boxes, 2):
+        row = jnp.concatenate([code_ref[b : b + 1], code_ref[b + 1 : b + 2]], axis=1)
+        hot = jnp.where(low_kinds == row, 1.0, 0.0).astype(BF16)
+        got = dot(table_ref[...], hot)
+        for u in range(2):
+            real = got[:kdir, u * width : (u + 1) * width]
+            imag = got[kdir:, u * width : (u + 1) * width]
+            op[pl.ds(b + u, kdir, stride=2 * boxes), :] = jnp.where(low_first, real, -imag)
+            op[pl.ds(boxes + b + u, kdir, stride=2 * boxes), :] = jnp.where(low_first, imag, real)
+
+    def operator(k):
+        return op[pl.ds(pl.multiple_of(k * 2 * boxes, 2 * boxes), 2 * boxes), :].astype(BF16)
 
     for chain in range(2):
         halve(chain, 0)
@@ -221,13 +255,13 @@
         return carry
 
     lax.fori_loop(1, n, take, 0)
-    parents2 = 2 * n * groups8
-
     def translate(t, carry):
         for u in range(unroll):
             q = t * unroll + u
             sources = wide[pl.ds(q, parents2, stride=qloc), :].astype(BF16)
-            result[pl.ds(q, parents2, stride=qloc), :] = dot(couple_ref[q], sources)
+            result[pl.ds(q, parents2, stride=qloc), :] = dot(
+                couple[pl.ds(pl.multiple_of(q * parents2, parents2), parents2), :].astype(BF16), sources
+            )
         return carry
 
     lax.fori_loop(0, qloc // unroll, translate, 0)
@@ -251,7 +285,23 @@
     lax.fori_loop(1, n, start_back, 0)
     returned[:, :, pl.ds(pl.multiple_of(me * qloc, qloc), qloc), :] = result_send[:, pl.ds(me * groups8, groups8)]
 
-    for depth in range(1, len(later)):
+    for chain in range(2):
+        halve(chain, 1)
+
+    for part in range(2):
+        for b in range(boxes):
+            own_wide[pl.ds((part * boxes + b) * kdir, kdir), :] = pat_ref[part, b].astype(F32)
+
+    def near_own(t, carry):
+        for u in range(unroll):
+            k = t * unroll + u
+            sources = own_wide[pl.ds(k, 2 * boxes, stride=kdir), :].astype(BF16)
+            out_ref[pl.ds(k, 2 * boxes, stride=kdir), :] = dot(operator(k)[:, : 2 * boxes], sources)
+        return carry
+
+    lax.fori_loop(0, kdir // unroll, near_own, 0)
+
+    for depth in range(2, len(later)):
         for chain in range(2):
             halve(chain, depth)
     for depth in range(len(later), 1, -1):
@@ -282,7 +332,7 @@
     for chain in range(2):
         double(chain, 1)
 
-    def near_half(part):
+    def near_half(part, at):
         def widen_far(j, carry):
             far_wide[pl.ds(pl.multiple_of(j * kdir, kdir), kdir), :] = far[part * half + j].astype(F32)
             return carry
@@ -294,21 +344,15 @@
                 k = t * unroll + u
                 sources = far_wide[pl.ds(k, half, stride=kdir), :].astype(BF16)
                 spots = pl.ds(k, 2 * boxes, stride=kdir)
-                out_ref[spots, :] = out_ref[spots, :] + dot(far_op_ref[part, k], sources)
+                out_ref[spots, :] = out_ref[spots, :] + dot(operator(k)[:, at : at + half], sources)
             return carry
 
         lax.fori_loop(0, kdir // unroll, near_far, 0)
 
-    near_half(me % 2)
+    near_half(me % 2, 2 * boxes)
     for chain in range(2):
         doubling(chain, 0).wait()
-    near_half(1 - me % 2)
-
-
-def block_complex(real, imag):
-    top = jnp.concatenate([real, -imag], axis=2)
-    bottom = jnp.concatenate([imag, real], axis=2)
-    return jnp.concatenate([top, bottom], axis=1)
+    near_half(1 - me % 2, 2 * boxes + half)
 
 
 def shards(
@@ -334,31 +378,14 @@
     rows = 2 * listed * 8
     sources = low_index.shape[1]
 
-    ntrans = low_table.shape[1]
-    kinds = jnp.arange(ntrans, dtype=jnp.int32)
-    low_code = jnp.where(low_mask > 0, low_index, -1)
-    low_hot = (low_code[:, :, None] == kinds).astype(BF16).reshape(boxes * sources, ntrans)
-    low_op = jnp.einsum("ctk,nt->ckn", low_table, low_hot, preferred_element_type=F32)
-    low_op = low_op.astype(BF16).reshape(2, kdir, boxes, sources)
-    own_op = block_complex(low_op[0, :, :, :boxes], low_op[1, :, :, :boxes])
-    far_real, far_imag = low_op[0, :, :, boxes:], low_op[1, :, :, boxes:]
-    far_op = jnp.stack(
-        [
-            jnp.concatenate([far_real, far_imag], axis=1),
-            jnp.concatenate([-far_imag, far_real], axis=1),
-        ]
-    )
-
+    code = jnp.where(low_mask > 0, low_index, -1)
+    own, listed_code = code[:, :boxes], code[:, boxes:]
+    spare = jnp.full((boxes, -2 * sources % 128), -1, jnp.int32)
+    code = jnp.concatenate([own, own, listed_code, listed_code, spare], axis=1)
+    low = jnp.transpose(low_table, (0, 2, 1)).reshape(2 * kdir, -1)
     start = lax.axis_index("box") * qloc
     table = lax.dynamic_slice_in_dim(par_table, start, qloc, 2)
-    match = par_source[:, :, None] == jnp.arange(parents, dtype=jnp.int32)
-    match = match & (par_mask[:, :, None] > 0)
-    par_code = jnp.sum(jnp.where(match, par_index[:, :, None] + 1, 0), axis=1) - 1
-    par_kinds = jnp.arange(par_table.shape[1], dtype=jnp.int32)
-    par_hot = (par_code[:, :, None] == par_kinds).astype(BF16).reshape(parents * parents, -1)
-    couple = jnp.einsum("ctq,nt->cqn", table, par_hot, preferred_element_type=F32)
-    couple = couple.astype(BF16).reshape(2, qloc, parents, parents)
-    couple = block_complex(couple[0], couple[1])
+    table = jnp.transpose(table, (0, 2, 1)).reshape(2 * qloc, -1)
 
     phase = jnp.concatenate([jnp.cos(shift_angle), jnp.sin(shift_angle)], axis=0).T
 
@@ -369,9 +396,11 @@
     return pl.pallas_call(
         functools.partial(kernel, n, listed),
         out_shape=jax.ShapeDtypeStruct((2 * boxes * kdir, illums), F32),
-        in_specs=[smem] + [vmem] * 7,
+        in_specs=[smem] + [vmem] * 9,
         out_specs=vmem,
         scratch_shapes=[
+            pltpu.VMEM((kdir * 2 * boxes, code.shape[1]), F32),
+            pltpu.VMEM((qloc * 2 * parents, 2 * parents), F32),
             pltpu.VMEM((2 * groups8, qdir, illums), BF16),
             pltpu.VMEM((n, 2 * groups8, qloc, illums), BF16),
             pltpu.VMEM((2 * parents * qloc, illums), F32),
@@ -395,7 +424,18 @@
         compiler_params=pltpu.CompilerParams(
             collective_id=0, has_side_effects=True, vmem_limit_bytes=56 * 1024 * 1024
         ),
-    )(owner_block, patterns, own_op, far_op, interp, interp.T, phase, couple).reshape(2, boxes, kdir, illums)
+    )(
+        owner_block,
+        patterns,
+        code,
+        low,
+        par_source,
+        par_index,
+        par_mask,
+        table,
+        interp,
+        phase,
+    ).reshape(2, boxes, kdir, illums)
 
 
 def solution(mesh):

time: 101 us -> 96.6 us (0.956)
  local copies, waits for them, and re-layouts: 14.2 us -> 11.8 us
  other arithmetic: 3.75 us -> 1.44 us
  Pallas kernels: 81.6 us -> 82.9 us
    another operation x1 -> x0, local copies, waits for them, and re-layouts: 3.65 us -> none  [shards(): jnp.stack([jnp.concatenate([far_real, far_imag], axis=1), jnp.concatenate...]
    transpose x0 -> x3, local copies, waits for them, and re-layouts: none -> 2.77 us  [the longest x1 1.77 us: shards(): low = jnp.transpose(low_table, (0, 2, 1)).reshape(2 * kdir, -1)]
    concatenate x1, local copies, waits for them, and re-layouts: 2.32 us -> 0.08 us  [shards(): code = jnp.concatenate([own, own, listed_code, listed_code, spare], axis=1)]
    unnamed x7 -> x6, local copies, waits for them, and re-layouts: 5.63 us -> 7.25 us
    pallas_call x1, Pallas kernels: 81.6 us -> 82.9 us  [shards(): pl.pallas_call(functools.partial(kernel, n, listed), out_shape=jax.ShapeD...]
where the time goes in v3:
time: 96.6 us; the launch traced here: 96.2 us
  Pallas kernels  82.9 us (86%)
  local copies, waits for them, and re-layouts  11.8 us (12%)
  other arithmetic  1.44 us (1%)
    pallas_call x1, Pallas kernels, shards(): pl.pallas_call(functools.partial(kernel, n, listed), out_shape=jax.ShapeD...  82.9 us
    unnamed x6, local copies, waits for them, and re-layouts  7.25 us

profile of v3, /device:TPU:0, one launch (start us, length us, event | category | flops | bytes accessed | tf_op | source)
XLA Modules:
  0.0 96.2 jit_solution(9948377087097966383)
XLA Ops:
  0.0 0.0 copy-start
  0.0 0.1 pad.5.clone
  0.1 0.8 compare_select_fusion
  0.8 0.1 slice.10
  0.9 0.7 add_add_fusion.code_ref
  1.6 1.4 %copy.22.source_ref = s32[32,16]{1,0:T(8,128)} copy(s32[32,16]{0,1:T(8,128)} %param.18) | data formatting | bytes 4096 | tf_op args[7]
  3.0 1.4 %copy.23.index_ref = s32[32,16]{1,0:T(8,128)} copy(s32[32,16]{0,1:T(8,128)} %param.19) | data formatting | bytes 4096 | tf_op args[8]
  4.3 1.4 %copy.24.mask_ref = s32[32,16]{1,0:T(8,128)} copy(s32[32,16]{0,1:T(8,128)} %param.20) | data formatting | bytes 4096 | tf_op args[9]
  5.7 0.8 fusion
  6.5 0.0 copy-done
  6.5 0.2 dynamic-slice_bitcast_fusion
  6.8 0.8 copy.20
  7.5 1.8 %copy.19 = bf16[2,128,316]{2,1,0:T(8,128)(2,1)} copy(bf16[2,128,316]{1,0,2:T(2,128)(2,1)} %bitcast.12) | data formatting | bytes 323584 | tf_op jit(solution)/shard_map/transpose | solution.py:385
  9.3 0.8 copy.21
  10.1 82.9 %shard_map.109 = f32[4096,128]{1,0:T(8,128)} custom-call(s32[4]{0:T(128)} %owner_ref.1, bf16[2,16,128,128]{3,2,1,0:T(8,128)(2,1)} %pat_ref.1, s32[16,128]{1,0:T(8,128)} %add_add_fusion.code_ref, bf16[256,316]{1,0:T(8,128)(2,1)} %bitcast.10, s32[32,16]{1,0:T(8,128)} %copy.22.source_ref, s32[32,16]{1,0:T(8,128)} %copy.23.index_ref, s32[32,16]{1,0:T(8,128)} %copy.24.mask_ref, ...), custom_call_target="tpu_custom_call" | custom-call | tf_op jit(solution)/shard_map/pallas_call | solution.py:396
  93.0 3.1 %copy.26 = f32[2,16,128,128]{3,2,1,0:T(8,128)} copy(f32[2,16,128,128]{3,2,1,0:T(8,128)} %bitcast.8) | data formatting | bytes 4194304
  (2 shorter events, 0.0 us)
Async XLA Ops:
  0.0 6.5 %copy-start = (bf16[2,316,512]{2,0,1:T(2,128)(2,1)S(1)}, bf16[2,316,512]{2,0,1:T(2,128)(2,1)}, u32[]{:S(2)}) copy-start(bf16[2,316,512]{2,0,1:T(2,128)(2,1)} %param.21) | copy-start | bytes 1941508

commit v4 on v3

--- a/solution.py
+++ b/solution.py
@@ -19,6 +19,7 @@
 def kernel(
     n,
     listed,
+    pitches,
     owner_ref,
     pat_ref,
     code_ref,
@@ -28,8 +29,9 @@
     mask_ref,
     par_ref,
     interp_ref,
+    angle_ref,
+    out_ref,
     phase_ref,
-    out_ref,
     op,
     couple,
     parent,
@@ -43,6 +45,7 @@
     far,
     far_wide,
     own_wide,
+    acc,
     out_send,
     out_recv,
     back_send,
@@ -60,6 +63,7 @@
     qloc = qdir // n
     rows = 2 * listed * 8
     stages = n.bit_length() - 1
+    kpitch, bpitch, qpitch, ppitch = pitches
 
     barrier = pltpu.get_barrier_semaphore()
 
@@ -146,6 +150,8 @@
         doubling(chain, depth - 1).start()
 
     first_swap().start()
+    phase_ref[:, :8] = jnp.cos(angle_ref[...]).T
+    phase_ref[:, 8:] = jnp.sin(angle_ref[...]).T
 
     tile = 256
     for parent_at in range(groups8):
@@ -192,15 +198,16 @@
     halving(0, 0).start()
     halving(1, 0).start()
 
-    unroll = 4
+    unroll = 8
     parents = n * groups8
     parents2 = 2 * parents
 
     lanes = lax.broadcasted_iota(jnp.int32, (parents, parents), 1)
     code = jnp.zeros((parents, parents), jnp.int32)
-    slot_code = jnp.where(mask_ref[...] > 0, index_ref[...] + 1, 0)
-    for j in range(source_ref.shape[1]):
-        code = code + jnp.where(source_ref[:, j : j + 1] == lanes, slot_code[:, j : j + 1], 0)
+    slot_code = jnp.where(mask_ref[...] > 0, index_ref[...] + 1, 0).T
+    slot_source = source_ref[...].T
+    for j in range(source_ref.shape[0]):
+        code = code + jnp.where(slot_source[:, j : j + 1] == lanes, slot_code[:, j : j + 1], 0)
     code = jnp.concatenate([code, code], axis=1) - 1
     each = max(1, 256 // parents2)
     kinds = lax.broadcasted_iota(jnp.int32, (par_ref.shape[1], each * parents2), 0)
@@ -212,8 +219,8 @@
         for u in range(each):
             real = got[:qloc, u * parents2 : (u + 1) * parents2]
             imag = got[qloc:, u * parents2 : (u + 1) * parents2]
-            couple[pl.ds(p + u, qloc, stride=parents2), :] = jnp.where(first, real, -imag)
-            couple[pl.ds(parents + p + u, qloc, stride=parents2), :] = jnp.where(first, imag, real)
+            couple[pl.ds(p + u, qloc, stride=ppitch), :] = jnp.where(first, real, -imag)
+            couple[pl.ds(parents + p + u, qloc, stride=ppitch), :] = jnp.where(first, imag, real)
 
     width = code_ref.shape[1]
     low_kinds = lax.broadcasted_iota(jnp.int32, (table_ref.shape[1], 2 * width), 0)
@@ -230,11 +237,11 @@
         for u in range(2):
             real = got[:kdir, u * width : (u + 1) * width]
             imag = got[kdir:, u * width : (u + 1) * width]
-            op[pl.ds(b + u, kdir, stride=2 * boxes), :] = jnp.where(low_first, real, -imag)
-            op[pl.ds(boxes + b + u, kdir, stride=2 * boxes), :] = jnp.where(low_first, imag, real)
+            op[pl.ds(b + u, kdir, stride=bpitch), :] = jnp.where(low_first, real, -imag)
+            op[pl.ds(boxes + b + u, kdir, stride=bpitch), :] = jnp.where(low_first, imag, real)
 
     def operator(k):
-        return op[pl.ds(pl.multiple_of(k * 2 * boxes, 2 * boxes), 2 * boxes), :].astype(BF16)
+        return op[pl.ds(pl.multiple_of(k * bpitch, 8), 2 * boxes), :].astype(BF16)
 
     for chain in range(2):
         halve(chain, 0)
@@ -243,7 +250,7 @@
         for part in range(2):
             for p in range(groups8):
                 s = (part * n + source) * groups8 + p
-                at = pl.multiple_of(s * qloc, qloc)
+                at = pl.multiple_of(s * qpitch, 8)
                 wide[pl.ds(at, qloc), :] = value(part * groups8 + p).astype(F32)
 
     widen(me, lambda c: parent[c, pl.ds(pl.multiple_of(me * qloc, qloc), qloc), :])
@@ -258,14 +265,15 @@
     def translate(t, carry):
         for u in range(unroll):
             q = t * unroll + u
-            sources = wide[pl.ds(q, parents2, stride=qloc), :].astype(BF16)
-            result[pl.ds(q, parents2, stride=qloc), :] = dot(
-                couple[pl.ds(pl.multiple_of(q * parents2, parents2), parents2), :].astype(BF16), sources
+            sources = wide[pl.ds(q, parents2, stride=qpitch), :].astype(BF16)
+            result[pl.ds(q, parents2, stride=qpitch), :] = dot(
+                couple[pl.ds(pl.multiple_of(q * ppitch, 8), parents2), :].astype(BF16), sources
             )
         return carry
 
     lax.fori_loop(0, qloc // unroll, translate, 0)
-    result_send[...] = result[...].reshape(2, n * groups8, qloc, illums).astype(BF16)
+    for s in range(parents2):
+        result_send[s // parents, s % parents] = result[pl.ds(s * qpitch, qloc), :].astype(BF16)
 
     def back_copy(i):
         peer = lax.rem(me + i, n)
@@ -290,13 +298,16 @@
 
     for part in range(2):
         for b in range(boxes):
-            own_wide[pl.ds((part * boxes + b) * kdir, kdir), :] = pat_ref[part, b].astype(F32)
+            own_wide[pl.ds((part * boxes + b) * kpitch, kdir), :] = pat_ref[part, b].astype(F32)
 
     def near_own(t, carry):
+        sums = []
         for u in range(unroll):
             k = t * unroll + u
-            sources = own_wide[pl.ds(k, 2 * boxes, stride=kdir), :].astype(BF16)
-            out_ref[pl.ds(k, 2 * boxes, stride=kdir), :] = dot(operator(k)[:, : 2 * boxes], sources)
+            sources = own_wide[pl.ds(k, 2 * boxes, stride=kpitch), :].astype(BF16)
+            sums.append(dot(operator(k)[:, : 2 * boxes], sources))
+        for u in range(unroll):
+            acc[pl.ds(t * unroll + u, 2 * boxes, stride=kpitch), :] = sums[u]
         return carry
 
     lax.fori_loop(0, kdir // unroll, near_own, 0)
@@ -325,26 +336,29 @@
             imag = (cosine * im - sine * re).astype(BF16)
             both = dot(interp_ref[...], jnp.concatenate([real, imag], axis=1))
             spots = pl.ds(b * kdir, kdir)
-            out_ref[spots, :] = out_ref[spots, :] + both[:, :illums]
+            out_ref[spots, :] = both[:, :illums]
             spots = pl.ds((boxes + b) * kdir, kdir)
-            out_ref[spots, :] = out_ref[spots, :] + both[:, illums:]
+            out_ref[spots, :] = both[:, illums:]
 
     for chain in range(2):
         double(chain, 1)
 
     def near_half(part, at):
         def widen_far(j, carry):
-            far_wide[pl.ds(pl.multiple_of(j * kdir, kdir), kdir), :] = far[part * half + j].astype(F32)
+            far_wide[pl.ds(pl.multiple_of(j * kpitch, 8), kdir), :] = far[part * half + j].astype(F32)
             return carry
 
         lax.fori_loop(0, half, widen_far, 0)
 
         def near_far(t, carry):
+            sums = []
             for u in range(unroll):
                 k = t * unroll + u
-                sources = far_wide[pl.ds(k, half, stride=kdir), :].astype(BF16)
-                spots = pl.ds(k, 2 * boxes, stride=kdir)
-                out_ref[spots, :] = out_ref[spots, :] + dot(operator(k)[:, at : at + half], sources)
+                sources = far_wide[pl.ds(k, half, stride=kpitch), :].astype(BF16)
+                spots = pl.ds(k, 2 * boxes, stride=kpitch)
+                sums.append(acc[spots, :] + dot(operator(k)[:, at : at + half], sources))
+            for u in range(unroll):
+                acc[pl.ds(t * unroll + u, 2 * boxes, stride=kpitch), :] = sums[u]
             return carry
 
         lax.fori_loop(0, kdir // unroll, near_far, 0)
@@ -353,6 +367,10 @@
     for chain in range(2):
         doubling(chain, 0).wait()
     near_half(1 - me % 2, 2 * boxes + half)
+
+    for b in range(2 * boxes):
+        spots = pl.ds(b * kdir, kdir)
+        out_ref[spots, :] = out_ref[spots, :] + acc[pl.ds(b * kpitch, kdir), :]
 
 
 def shards(
@@ -387,31 +405,33 @@
     table = lax.dynamic_slice_in_dim(par_table, start, qloc, 2)
     table = jnp.transpose(table, (0, 2, 1)).reshape(2 * qloc, -1)
 
-    phase = jnp.concatenate([jnp.cos(shift_angle), jnp.sin(shift_angle)], axis=0).T
-
+    pitches = (kdir + 8, 2 * boxes + 8, qloc + 8, 2 * parents + 8)
+    kpitch, bpitch, qpitch, ppitch = pitches
     vmem = pl.BlockSpec(memory_space=pltpu.VMEM)
     smem = pl.BlockSpec(memory_space=pltpu.SMEM)
     stages = n.bit_length() - 1
     dma = pltpu.SemaphoreType.DMA
     return pl.pallas_call(
-        functools.partial(kernel, n, listed),
+        functools.partial(kernel, n, listed, pitches),
         out_shape=jax.ShapeDtypeStruct((2 * boxes * kdir, illums), F32),
         in_specs=[smem] + [vmem] * 9,
         out_specs=vmem,
         scratch_shapes=[
-            pltpu.VMEM((kdir * 2 * boxes, code.shape[1]), F32),
-            pltpu.VMEM((qloc * 2 * parents, 2 * parents), F32),
+            pltpu.VMEM((qdir, 16), F32),
+            pltpu.VMEM((kdir * bpitch, code.shape[1]), F32),
+            pltpu.VMEM((qloc * ppitch, 2 * parents), F32),
             pltpu.VMEM((2 * groups8, qdir, illums), BF16),
             pltpu.VMEM((n, 2 * groups8, qloc, illums), BF16),
-            pltpu.VMEM((2 * parents * qloc, illums), F32),
-            pltpu.VMEM((2 * parents * qloc, illums), F32),
+            pltpu.VMEM((2 * parents * qpitch, illums), F32),
+            pltpu.VMEM((2 * parents * qpitch, illums), F32),
             pltpu.VMEM((2, parents, qloc, illums), BF16),
             pltpu.VMEM((2, groups8, qdir, illums), BF16),
             pltpu.VMEM((rows, kdir, illums), BF16),
             pltpu.VMEM((rows, kdir, illums), BF16),
             pltpu.VMEM((rows, kdir, illums), BF16),
-            pltpu.VMEM((rows // 2 * kdir, illums), F32),
-            pltpu.VMEM((2 * boxes * kdir, illums), F32),
+            pltpu.VMEM((rows // 2 * kpitch, illums), F32),
+            pltpu.VMEM((2 * boxes * kpitch, illums), F32),
+            pltpu.VMEM((2 * boxes * kpitch, illums), F32),
             dma((n,)),
             dma((n,)),
             dma((n,)),
@@ -429,12 +449,12 @@
         patterns,
         code,
         low,
-        par_source,
-        par_index,
-        par_mask,
+        par_source.T,
+        par_index.T,
+        par_mask.T,
         table,
         interp,
-        phase,
+        shift_angle,
     ).reshape(2, boxes, kdir, illums)
 
 

time: 96.6 us -> 82.7 us (0.86)
  Pallas kernels: 82.9 us -> 74.9 us
  local copies, waits for them, and re-layouts: 11.8 us -> 6.03 us
    pallas_call x1, Pallas kernels: 82.9 us -> 74.9 us  [shards(): pl.pallas_call(functools.partial(kernel, n, listed, pitches), out_shape=j...]
    unnamed x6 -> x3, local copies, waits for them, and re-layouts: 7.25 us -> 3.14 us
where the time goes in v4:
time: 82.7 us; the launch traced here: 82.4 us
  Pallas kernels  74.9 us (91%)
  local copies, waits for them, and re-layouts  6.03 us (7%)
  other arithmetic  1.44 us (2%)
    pallas_call x1, Pallas kernels, shards(): pl.pallas_call(functools.partial(kernel, n, listed, pitches), out_shape=j...  74.9 us
    unnamed x3, local copies, waits for them, and re-layouts  3.14 us
    transpose x1, local copies, waits for them, and re-layouts, shards(): low = jnp.transpose(low_table, (0, 2, 1)).reshape(2 * kdir, -1)  1.74 us

profile of v4, /device:TPU:0, one launch (start us, length us, event | category | flops | bytes accessed | tf_op | source)
XLA Modules:
  0.0 82.4 jit_solution(3620261191129111772)
XLA Ops:
  0.0 0.0 copy-start
  0.0 0.1 pad.3.clone
  0.1 0.8 compare_select_fusion
  0.8 0.1 slice.10
  0.9 0.7 add_add_fusion.code_ref
  1.6 0.0 copy-done
  1.6 0.2 dynamic-slice_bitcast_fusion
  1.8 0.8 copy.13
  2.6 1.7 %copy.12 = bf16[2,128,316]{2,1,0:T(8,128)(2,1)} copy(bf16[2,128,316]{1,0,2:T(2,128)(2,1)} %bitcast.13) | data formatting | bytes 323584 | tf_op jit(solution)/shard_map/transpose | solution.py:403
  4.3 74.9 %shard_map.109 = f32[4096,128]{1,0:T(8,128)} custom-call(s32[4]{0:T(128)} %owner_ref.1, bf16[2,16,128,128]{3,2,1,0:T(8,128)(2,1)} %pat_ref.1, s32[16,128]{1,0:T(8,128)} %add_add_fusion.code_ref, bf16[256,316]{1,0:T(8,128)(2,1)} %bitcast.11, s32[16,32]{1,0:T(8,128)} %bitcast.15, s32[16,32]{1,0:T(8,128)} %bitcast.16, s32[16,32]{1,0:T(8,128)} %bitcast.17, ...), custom_call_target="tpu_custom_call" | custom-call | tf_op jit(solution)/shard_map/pallas_call | solution.py:414
  79.2 3.1 %copy.15 = f32[2,16,128,128]{3,2,1,0:T(8,128)} copy(f32[2,16,128,128]{3,2,1,0:T(8,128)} %bitcast.10) | data formatting | bytes 4194304
  (1 shorter events, 0.0 us)
Async XLA Ops:
  0.0 1.6 %copy-start = (bf16[2,316,512]{2,0,1:T(2,128)(2,1)S(1)}, bf16[2,316,512]{2,0,1:T(2,128)(2,1)}, u32[]{:S(2)}) copy-start(bf16[2,316,512]{2,0,1:T(2,128)(2,1)} %param.21) | copy-start | bytes 1941508
